TPU v7x, 32 devices: a whole 2x2x4 slice. The times are simulated.
32 devices in a mesh: dp: 8 (over z, y), mp: 4 (over x, core).
Axes of the slice: x: 2, y: 2, z: 4, core: 2. Of those that a mesh axis runs over, the one named last changes fastest.
Arguments:
- tokens: bfloat16 [4096, 2048], P('dp'), may hold values from -6 to 6
- text: bfloat16 [2048, 4096], P('dp', 'mp'), may hold values from -6 to 6
- image_seg: int32 [8, 512], P('dp'), may hold values from 0 to 1, never falling along the last dimension, each value on 1 to 320 neighbouring positions
- text_seg: int32 [8, 256], P('dp'), may hold values from 0 to 1, never falling along the last dimension, each value on 1 to 160 neighbouring positions
- w_qkv: bfloat16 [3, 2048, 2048], P(None, 'dp', 'mp'), may hold values from -0.125 to 0.125
- w_out: bfloat16 [2048, 2048], P('mp', 'dp'), may hold values from -1 to 1
- c_q: bfloat16 [2048, 2048], P('dp', 'mp'), may hold values from -0.125 to 0.125
- c_kv: bfloat16 [2, 4096, 2048], P(None, 'dp', 'mp'), may hold values from -0.09375 to 0.09375
- c_out: bfloat16 [2048, 2048], P('mp', 'dp'), may hold values from -1 to 1
- w_up: bfloat16 [2048, 8192], P('dp', 'mp'), may hold values from -0.125 to 0.125
- w_down: bfloat16 [8192, 2048], P('mp', 'dp'), may hold values from -0.0625 to 0.0625
- norm_gain: float32 [4, 2048], replicated, may hold values from 0.25 to 1.75
- norm_bias: float32 [4, 2048], replicated, may hold values from -4 to 4
- out_bias: float32 [3, 2048], replicated, may hold values from -4 to 4
- up_bias: float32 [8192], P('mp'), may hold values from -4 to 4
- cotangent: bfloat16 [4096, 2048], P('dp'), may hold values from -6 to 6
Outputs:
- output: bfloat16 [4096, 2048], P('dp')
- grad_tokens: float32 [4096, 2048], P('dp')
- grad_text: float32 [2048, 4096], P('dp', 'mp')
- grad_w_qkv: float32 [3, 2048, 2048], P(None, 'dp', 'mp')
- grad_w_out: float32 [2048, 2048], P('mp', 'dp')
- grad_c_q: float32 [2048, 2048], P('dp', 'mp')
- grad_c_kv: float32 [2, 4096, 2048], P(None, 'dp', 'mp')
- grad_c_out: float32 [2048, 2048], P('mp', 'dp')
- grad_w_up: float32 [2048, 8192], P('dp', 'mp')
- grad_w_down: float32 [8192, 2048], P('mp', 'dp')
- grad_norm_gain: float32 [4, 2048], replicated
- grad_norm_bias: float32 [4, 2048], replicated
- grad_out_bias: float32 [3, 2048], replicated
- grad_up_bias: float32 [8192], P('mp')
Inputs may be any that keep to these rules, and one draw needn't show every extreme that they name: In each row image_seg is 0 on the first image and 1 on the second; both images are present, and none has more than 320 tokens. In each row text_seg is 0 on the first caption and 1 on the second; both captions are present, and none has more than 160 tokens.
All inputs are finite; a program needn't handle non-finite values.
Results may differ from a plain program's by a relative error of at most 0.02.
Values may be sent and summed in bfloat16 or wider, within the bound.
No kernel may reach another device: no remote copies, remote signals or barrier semaphores. Data moves between devices by JAX's collectives and lax.ppermute only.
A program may use at most 256 MiB of HBM per device.

v0:
```python
import jax
import jax.numpy as jnp
from jax import lax
from jax.sharding import PartitionSpec as P

HD = 128
eps = 1e-05
masked = -1e30


def normalize(values, gain, shift):
    center = values - jnp.mean(values, axis=-1, keepdims=True)
    spread = jnp.mean(center * center, axis=-1, keepdims=True)
    return center * lax.rsqrt(spread + eps) * gain + shift


def gelu_tanh(values):
    return (
        0.5
        * values
        * (1.0 + jnp.tanh(0.7978845608028654 * (values + 0.044715 * values * values * values)))
    )


def heads_sum(partial_value):
    return lax.psum(partial_value, "mp")


def input_sum(partial_value):
    return lax.psum(partial_value, "mp")


def split_heads(values):
    return values.reshape(values.shape[0], values.shape[1] // HD, HD)


def scores_of(queries, key_rows, allowed):
    raw = jnp.einsum(
        "qhd,khd->hqk",
        split_heads(queries),
        split_heads(key_rows),
        preferred_element_type=jnp.float32,
    ) * HD ** (-0.5)
    return jnp.where(allowed[None], raw, masked)


def attend_forward(queries, key_rows, value_rows, allowed):
    scores = scores_of(queries, key_rows, allowed)
    top = jnp.max(scores, axis=-1, keepdims=True)
    expo = jnp.exp(scores - top)
    total = jnp.sum(expo, axis=-1, keepdims=True)
    probs = (expo / total).astype(jnp.bfloat16)
    mixed = jnp.einsum(
        "hqk,khd->qhd", probs, split_heads(value_rows), preferred_element_type=jnp.float32
    )
    return (
        mixed.reshape(queries.shape[0], queries.shape[1]).astype(jnp.bfloat16),
        top + jnp.log(total),
    )


def attend_backward(queries, key_rows, value_rows, grad_mixed, logsum, allowed):
    scores = scores_of(queries, key_rows, allowed)
    probs = jnp.exp(scores - logsum)
    grad_heads = split_heads(grad_mixed)
    grad_values = jnp.einsum(
        "hqk,qhd->khd", probs.astype(jnp.bfloat16), grad_heads, preferred_element_type=jnp.float32
    )
    grad_probs = jnp.einsum(
        "qhd,khd->hqk", grad_heads, split_heads(value_rows), preferred_element_type=jnp.float32
    )
    grad_scores = (
        probs * (grad_probs - jnp.sum(probs * grad_probs, axis=-1, keepdims=True))
    ).astype(jnp.bfloat16)
    grad_queries = jnp.einsum(
        "hqk,khd->qhd", grad_scores, split_heads(key_rows), preferred_element_type=jnp.float32
    ) * HD ** (-0.5)
    grad_keys = jnp.einsum(
        "hqk,qhd->khd", grad_scores, split_heads(queries), preferred_element_type=jnp.float32
    ) * HD ** (-0.5)
    return (
        grad_queries.reshape(queries.shape),
        grad_keys.reshape(key_rows.shape),
        grad_values.reshape(value_rows.shape),
    )


def on_device(
    tokens,
    text,
    image_seg,
    text_seg,
    w_qkv,
    w_out,
    c_q,
    c_kv,
    c_out,
    w_up,
    w_down,
    norm_gain,
    norm_bias,
    out_bias,
    up_bias,
    cotangent,
):
    row_count = image_seg.shape[0]
    length = image_seg.shape[1]
    text_len = text_seg.shape[1]
    gathered = (
        lax.all_gather(w_qkv, "dp", axis=1, tiled=True),
        lax.all_gather(w_out, "dp", axis=1, tiled=True),
        lax.all_gather(c_q, "dp", axis=0, tiled=True),
        lax.all_gather(c_kv, "dp", axis=1, tiled=True),
        lax.all_gather(c_out, "dp", axis=1, tiled=True),
        lax.all_gather(w_up, "dp", axis=0, tiled=True),
        lax.all_gather(w_down, "dp", axis=1, tiled=True),
    )
    full_qkv, full_out, full_cq, full_ckv, full_cout, full_up, full_down = gathered
    words = lax.all_gather(text, "mp", axis=1, tiled=True)
    same_image = image_seg[:, :, None] == image_seg[:, None, :]
    caption = image_seg[:, :, None] == text_seg[:, None, :]
    residual = tokens.astype(jnp.float32)
    width = full_qkv.shape[2]
    normed_one, pull_one = jax.vjp(normalize, residual, norm_gain[0], norm_bias[0])
    hidden_one = normed_one.astype(jnp.bfloat16)
    projected = jnp.einsum(
        "td,cde->cte", hidden_one, full_qkv, preferred_element_type=jnp.float32
    ).astype(jnp.bfloat16)
    self_inputs = (
        projected[0].reshape(row_count, length, width),
        projected[1].reshape(row_count, length, width),
        projected[2].reshape(row_count, length, width),
    )
    self_mixed, self_logsum = lax.map(
        lambda pieces: attend_forward(*pieces), self_inputs + (same_image,)
    )
    self_flat = self_mixed.reshape(row_count * length, width)
    after_self = (
        residual
        + heads_sum(jnp.dot(self_flat, full_out, preferred_element_type=jnp.float32))
        + out_bias[0]
    )
    normed_two, pull_two = jax.vjp(normalize, after_self, norm_gain[1], norm_bias[1])
    hidden_two = normed_two.astype(jnp.bfloat16)
    cross_query = jnp.dot(hidden_two, full_cq, preferred_element_type=jnp.float32).astype(
        jnp.bfloat16
    )
    text_kv = jnp.einsum("td,cde->cte", words, full_ckv, preferred_element_type=jnp.float32).astype(
        jnp.bfloat16
    )
    cross_inputs = (
        cross_query.reshape(row_count, length, width),
        text_kv[0].reshape(row_count, text_len, width),
        text_kv[1].reshape(row_count, text_len, width),
    )
    cross_mixed, cross_logsum = lax.map(
        lambda pieces: attend_forward(*pieces), cross_inputs + (caption,)
    )
    cross_flat = cross_mixed.reshape(row_count * length, width)
    after_cross = (
        after_self
        + heads_sum(jnp.dot(cross_flat, full_cout, preferred_element_type=jnp.float32))
        + out_bias[1]
    )
    normed_three, pull_three = jax.vjp(normalize, after_cross, norm_gain[2], norm_bias[2])
    hidden_three = normed_three.astype(jnp.bfloat16)
    pre_act = jnp.dot(hidden_three, full_up, preferred_element_type=jnp.float32) + up_bias
    activated, pull_gelu = jax.vjp(gelu_tanh, pre_act)
    act_low = activated.astype(jnp.bfloat16)
    after_mlp = (
        after_cross
        + heads_sum(jnp.dot(act_low, full_down, preferred_element_type=jnp.float32))
        + out_bias[2]
    )
    final, pull_four = jax.vjp(normalize, after_mlp, norm_gain[3], norm_bias[3])
    output = final.astype(jnp.bfloat16)
    grad_mlp, gain_four, shift_four = pull_four(cotangent.astype(jnp.float32))
    grad_mlp_low = grad_mlp.astype(jnp.bfloat16)
    grad_down = jnp.einsum("tf,td->fd", act_low, grad_mlp_low, preferred_element_type=jnp.float32)
    grad_act = jnp.einsum("td,fd->tf", grad_mlp_low, full_down, preferred_element_type=jnp.float32)
    grad_pre = pull_gelu(grad_act)[0].astype(jnp.bfloat16)
    up_bias_grad = jnp.sum(grad_pre.astype(jnp.float32), axis=0)
    grad_up = jnp.einsum("td,tf->df", hidden_three, grad_pre, preferred_element_type=jnp.float32)
    grad_hidden_three = input_sum(
        jnp.einsum("tf,df->td", grad_pre, full_up, preferred_element_type=jnp.float32)
    )
    grad_cross_in, gain_three, shift_three = pull_three(grad_hidden_three)
    grad_after_cross = grad_mlp + grad_cross_in
    grad_cross_low = grad_after_cross.astype(jnp.bfloat16)
    grad_cout = jnp.einsum(
        "te,td->ed", cross_flat, grad_cross_low, preferred_element_type=jnp.float32
    )
    grad_cmix = jnp.einsum(
        "td,ed->te", grad_cross_low, full_cout, preferred_element_type=jnp.float32
    ).astype(jnp.bfloat16)
    cq_grad, ck_grad, cv_grad = lax.map(
        lambda pieces: attend_backward(*pieces),
        cross_inputs + (grad_cmix.reshape(row_count, length, width), cross_logsum, caption),
    )
    cq_low = cq_grad.reshape(row_count * length, width).astype(jnp.bfloat16)
    ckv_low = jnp.stack(
        [ck_grad.reshape(row_count * text_len, width), cv_grad.reshape(row_count * text_len, width)]
    ).astype(jnp.bfloat16)
    grad_cq = jnp.einsum("td,te->de", hidden_two, cq_low, preferred_element_type=jnp.float32)
    grad_ckv = jnp.einsum("td,cte->cde", words, ckv_low, preferred_element_type=jnp.float32)
    text_term = jnp.einsum("cte,cde->td", ckv_low, full_ckv, preferred_element_type=jnp.float32)
    grad_text = lax.psum_scatter(
        text_term.astype(jnp.bfloat16), "mp", scatter_dimension=1, tiled=True
    ).astype(jnp.float32)
    grad_hidden_two = input_sum(
        jnp.einsum("te,de->td", cq_low, full_cq, preferred_element_type=jnp.float32)
    )
    grad_self_in, gain_two, shift_two = pull_two(grad_hidden_two)
    grad_after_self = grad_after_cross + grad_self_in
    grad_self_low = grad_after_self.astype(jnp.bfloat16)
    grad_wout = jnp.einsum(
        "te,td->ed", self_flat, grad_self_low, preferred_element_type=jnp.float32
    )
    grad_smix = jnp.einsum(
        "td,ed->te", grad_self_low, full_out, preferred_element_type=jnp.float32
    ).astype(jnp.bfloat16)
    sq_grad, sk_grad, sv_grad = lax.map(
        lambda pieces: attend_backward(*pieces),
        self_inputs + (grad_smix.reshape(row_count, length, width), self_logsum, same_image),
    )
    qkv_low = jnp.stack(
        [
            sq_grad.reshape(row_count * length, width),
            sk_grad.reshape(row_count * length, width),
            sv_grad.reshape(row_count * length, width),
        ]
    ).astype(jnp.bfloat16)
    grad_qkv = jnp.einsum("td,cte->cde", hidden_one, qkv_low, preferred_element_type=jnp.float32)
    grad_hidden_one = input_sum(
        jnp.einsum("cte,cde->td", qkv_low, full_qkv, preferred_element_type=jnp.float32)
    )
    grad_in_one, gain_one, shift_one = pull_one(grad_hidden_one)
    grad_tokens = grad_after_self + grad_in_one
    gain_terms = jnp.stack([gain_one, gain_two, gain_three, gain_four])
    shift_terms = jnp.stack([shift_one, shift_two, shift_three, shift_four])
    bias_terms = jnp.stack(
        [
            jnp.sum(grad_after_self, axis=0),
            jnp.sum(grad_after_cross, axis=0),
            jnp.sum(grad_mlp, axis=0),
        ]
    )
    gain_total, shift_total, bias_total, up_total = (
        lax.psum(gain_terms.astype(jnp.bfloat16), "dp").astype(jnp.float32),
        lax.psum(shift_terms.astype(jnp.bfloat16), "dp").astype(jnp.float32),
        lax.psum(bias_terms.astype(jnp.bfloat16), "dp").astype(jnp.float32),
        lax.psum(up_bias_grad.astype(jnp.bfloat16), "dp").astype(jnp.float32),
    )
    sum_qkv, sum_wout, sum_cq, sum_ckv, sum_cout, sum_up, sum_down = (
        lax.psum_scatter(
            grad_qkv.astype(jnp.bfloat16), "dp", scatter_dimension=1, tiled=True
        ).astype(jnp.float32),
        lax.psum_scatter(
            grad_wout.astype(jnp.bfloat16), "dp", scatter_dimension=1, tiled=True
        ).astype(jnp.float32),
        lax.psum_scatter(
            grad_cq.astype(jnp.bfloat16), "dp", scatter_dimension=0, tiled=True
        ).astype(jnp.float32),
        lax.psum_scatter(
            grad_ckv.astype(jnp.bfloat16), "dp", scatter_dimension=1, tiled=True
        ).astype(jnp.float32),
        lax.psum_scatter(
            grad_cout.astype(jnp.bfloat16), "dp", scatter_dimension=1, tiled=True
        ).astype(jnp.float32),
        lax.psum_scatter(
            grad_up.astype(jnp.bfloat16), "dp", scatter_dimension=0, tiled=True
        ).astype(jnp.float32),
        lax.psum_scatter(
            grad_down.astype(jnp.bfloat16), "dp", scatter_dimension=1, tiled=True
        ).astype(jnp.float32),
    )
    return (
        output,
        grad_tokens,
        grad_text,
        sum_qkv,
        sum_wout,
        sum_cq,
        sum_ckv,
        sum_cout,
        sum_up,
        sum_down,
        gain_total,
        shift_total,
        bias_total,
        up_total,
    )


def solution(mesh):
    in_specs = (
        P("dp", None),
        P("dp", "mp"),
        P("dp", None),
        P("dp", None),
        P(None, "dp", "mp"),
        P("mp", "dp"),
        P("dp", "mp"),
        P(None, "dp", "mp"),
        P("mp", "dp"),
        P("dp", "mp"),
        P("mp", "dp"),
        P(),
        P(),
        P(),
        P("mp"),
        P("dp", None),
    )
    out_specs = (
        P("dp", None),
        P("dp", None),
        P("dp", "mp"),
        P(None, "dp", "mp"),
        P("mp", "dp"),
        P("dp", "mp"),
        P(None, "dp", "mp"),
        P("mp", "dp"),
        P("dp", "mp"),
        P("mp", "dp"),
        P(),
        P(),
        P(),
        P("mp"),
    )
    return jax.shard_map(
        on_device, mesh=mesh, in_specs=in_specs, out_specs=out_specs, check_vma=False
    )
```

profile of v0, /device:TPU:0, one launch (start us, length us, event | category | flops | bytes accessed | tf_op | source)
XLA Modules:
  0.0 2109.8 jit_solution(6485817762568258638)
XLA Ops:
  13.9 99.0 %all-gather.9.cloned.1.call-done = bf16[3,2048,512]{1,2,0:T(8,128)(2,1)} async-done(((bf16[3,256,512]{1,2,0:T(8,128)(2,1)}), bf16[3,2048,512]{1,2,0:T(8,128)(2,1)}) %all-gather.9.cloned.1.call-update) | async-done | bytes 6291472 | tf_op jit(solution)/shard_map/all_gather | solution.py:110
  112.9 6.5 fusion.35
  124.3 39.2 %all-gather.11.cloned.1.call-done = bf16[512,2048]{1,0:T(8,128)(2,1)} async-done(((bf16[512,256]{1,0:T(8,128)(2,1)}), bf16[512,2048]{1,0:T(8,128)(2,1)}) %all-gather.11.cloned.1.call-update) | async-done | bytes 2097168 | tf_op jit(solution)/shard_map/all_gather | solution.py:111
  163.5 4.9 fusion.88
  172.5 79.7 %all-reduce.8.cloned.1.call-done = f32[512,2048]{1,0:T(8,128)} async-done(((f32[512,2048]{1,0:T(8,128)}), f32[512,2048]{1,0:T(8,128)}) %all-reduce.8.cloned.1.call-update) | async-done | bytes 4194320 | tf_op jit(solution)/shard_map/psum | solution.py:26
  257.8 45.6 %all-gather.17.cloned.1.call-done = bf16[2048,512]{1,0:T(8,128)(2,1)} async-done(((bf16[256,512]{1,0:T(8,128)(2,1)}), bf16[2048,512]{1,0:T(8,128)(2,1)}) %all-gather.17.cloned.1.call-update) | async-done | bytes 2097168 | tf_op jit(solution)/shard_map/all_gather | solution.py:112
  306.4 19.6 all-gather.15.cloned.1.call-done
  326.0 127.4 %all-gather.13.cloned.1.call-done = bf16[2,4096,512]{1,2,0:T(8,128)(2,1)} async-done(((bf16[2,512,512]{1,2,0:T(8,128)(2,1)}), bf16[2,4096,512]{1,2,0:T(8,128)(2,1)}) %all-gather.13.cloned.1.call-update) | async-done | bytes 8388624 | tf_op jit(solution)/shard_map/all_gather | solution.py:113
  453.4 6.3 fusion.46
  461.3 42.8 %all-gather.19.cloned.1.call-done = bf16[512,2048]{1,0:T(8,128)(2,1)} async-done(((bf16[512,256]{1,0:T(8,128)(2,1)}), bf16[512,2048]{1,0:T(8,128)(2,1)}) %all-gather.19.cloned.1.call-update) | async-done | bytes 2097168 | tf_op jit(solution)/shard_map/all_gather | solution.py:114
  504.0 4.8 fusion.89
  510.5 82.3 %all-reduce.10.cloned.1.call-done = f32[512,2048]{1,0:T(8,128)} async-done(((f32[512,2048]{1,0:T(8,128)}), f32[512,2048]{1,0:T(8,128)}) %all-reduce.10.cloned.1.call-update) | async-done | bytes 4194320 | tf_op jit(solution)/shard_map/psum | solution.py:26
  592.7 4.0 fusion.77
  599.3 120.2 %all-gather.21.cloned.1.call-done = bf16[2048,2048]{1,0:T(8,128)(2,1)} async-done(((bf16[256,2048]{1,0:T(8,128)(2,1)}), bf16[2048,2048]{1,0:T(8,128)(2,1)}) %all-gather.21.cloned.1.call-update) | async-done | bytes 8388624 | tf_op jit(solution)/shard_map/all_gather | solution.py:115
  719.5 11.2 fusion.69
  730.7 113.8 %all-gather.23.cloned.1.call-done = bf16[2048,2048]{1,0:T(8,128)(2,1)} async-done(((bf16[2048,256]{1,0:T(8,128)(2,1)}), bf16[2048,2048]{1,0:T(8,128)(2,1)}) %all-gather.23.cloned.1.call-update) | async-done | bytes 8388624 | tf_op jit(solution)/shard_map/all_gather | solution.py:116
  844.5 11.5 fusion.68
  856.4 83.6 %all-reduce.12.cloned.1.call-done = f32[512,2048]{1,0:T(8,128)} async-done(((f32[512,2048]{1,0:T(8,128)}), f32[512,2048]{1,0:T(8,128)}) %all-reduce.12.cloned.1.call-update) | async-done | bytes 4194320 | tf_op jit(solution)/shard_map/psum | solution.py:26
  939.9 4.0 fusion.76
  947.0 2.9 fusion.75
  950.0 12.0 fusion.87
  963.3 6.1 fusion.90
  969.7 85.5 %all-reduce.14.cloned.1.call-done = f32[512,2048]{1,0:T(8,128)} async-done(((f32[512,2048]{1,0:T(8,128)}), f32[512,2048]{1,0:T(8,128)}) %all-reduce.14.cloned.1.call-update) | async-done | bytes 4194320 | tf_op jit(solution)/shard_map/psum | solution.py:30
  1055.2 4.8 multiply_reduce_fusion
  1068.6 3.3 fusion.91
  1072.5 85.2 %all-reduce.16.cloned.1.call-done = f32[512,2048]{1,0:T(8,128)} async-done(((f32[512,2048]{1,0:T(8,128)}), f32[512,2048]{1,0:T(8,128)}) %all-reduce.16.cloned.1.call-update) | async-done | bytes 4194320 | tf_op jit(solution)/shard_map/psum | solution.py:30
  1157.7 4.7 multiply_reduce_fusion.1
  1183.2 8.6 convolution_bitcast_fusion.1
  1191.9 4.3 convolution_convert_fusion.3
  1201.5 7.2 fusion.4
  1208.8 4.9 convolution_convert_fusion.2
  1213.8 4.8 convolution_convert_fusion.4
  1218.7 12.4 convolution_convert_fusion
  1232.7 9.4 convolution_convert_fusion.1
  1244.1 7.1 convert_bitcast_fusion.1
  1251.2 7.2 convert_bitcast_fusion
  1260.7 16.9 all-reduce.18.cloned.1.call-done
  1277.6 3.3 fusion.70
  1283.1 38.6 %all-reduce = (bf16[4,2048]{1,0:T(4,128)(2,1)S(1)}, bf16[4,2048]{1,0:T(4,128)(2,1)S(1)}, bf16[3,2048]{1,0:T(4,128)(2,1)S(1)}, bf16[2048]{0:T(1024)(128)(2,1)S(1)}) all-reduce(bf16[4,2048]{1,0:T(4,128)(2,1)S(1)} %get-tuple-element.190, bf16[4,2048]{1,0:T(4,128)(2,1)S(1)} %get-tuple-element.191, ...), channel_id=1, replica_groups=mesh['dp'=8,'mp'=4] {'dp'}, use_global_device_ids=true, to_apply=%region_40.41 | all-reduce | flops 24576 | bytes 98304 | tf_op jit(solution)/shard_map/psum | solution.py:249
  1324.2 5.6 add_add_fusion.4
  1329.8 20.3 reduce-scatter.15.cloned.1.call-done
  1352.0 31.5 %reduce-scatter.9.cloned.1.call-done = bf16[256,1024]{1,0:T(8,128)(2,1)} async-done(((bf16[256,4096]{1,0:T(8,128)(2,1)}), bf16[256,1024]{1,0:T(8,128)(2,1)}) %reduce-scatter.9.cloned.1.call-update) | async-done | bytes 524304 | tf_op jit(solution)/shard_map/reduce_scatter | solution.py:207
  1385.6 70.2 %reduce-scatter.19.cloned.1.call-done = bf16[512,256]{1,0:T(8,128)(2,1)} async-done(((bf16[512,2048]{1,0:T(8,128)(2,1)}), bf16[512,256]{1,0:T(8,128)(2,1)}) %reduce-scatter.19.cloned.1.call-update) | async-done | bytes 262160 | tf_op jit(solution)/shard_map/reduce_scatter | solution.py:267
  1457.5 70.0 %reduce-scatter.13.cloned.1.call-done = bf16[512,256]{1,0:T(8,128)(2,1)} async-done(((bf16[512,2048]{1,0:T(8,128)(2,1)}), bf16[512,256]{1,0:T(8,128)(2,1)}) %reduce-scatter.13.cloned.1.call-update) | async-done | bytes 262160 | tf_op jit(solution)/shard_map/reduce_scatter | solution.py:258
  1529.3 148.7 %reduce-scatter.23.cloned.1.call-done = bf16[2048,256]{1,0:T(8,128)(2,1)} async-done(((bf16[2048,2048]{1,0:T(8,128)(2,1)}), bf16[2048,256]{1,0:T(8,128)(2,1)}) %reduce-scatter.23.cloned.1.call-update) | async-done | bytes 1048592 | tf_op jit(solution)/shard_map/reduce_scatter | solution.py:273
  1680.8 147.4 %reduce-scatter.21.cloned.1.call-done = bf16[256,2048]{1,0:T(8,128)(2,1)} async-done(((bf16[2048,2048]{1,0:T(8,128)(2,1)}), bf16[256,2048]{1,0:T(8,128)(2,1)}) %reduce-scatter.21.cloned.1.call-update) | async-done | bytes 1048592 | tf_op jit(solution)/shard_map/reduce_scatter | solution.py:270
  1830.9 118.5 %reduce-scatter.11.cloned.1.call-done = bf16[3,256,512]{1,2,0:T(8,128)(2,1)} async-done(((bf16[3,2048,512]{1,2,0:T(8,128)(2,1)}), bf16[3,256,512]{1,2,0:T(8,128)(2,1)}) %reduce-scatter.11.cloned.1.call-update) | async-done | bytes 786448 | tf_op jit(solution)/shard_map/reduce_scatter | solution.py:255
  1951.9 148.2 %reduce-scatter.17.cloned.1.call-done = bf16[2,512,512]{1,2,0:T(8,128)(2,1)} async-done(((bf16[2,4096,512]{1,2,0:T(8,128)(2,1)}), bf16[2,512,512]{1,2,0:T(8,128)(2,1)}) %reduce-scatter.17.cloned.1.call-update) | async-done | bytes 1048592 | tf_op jit(solution)/shard_map/reduce_scatter | solution.py:264
  (249 shorter events, 98.0 us)
Async XLA Ops:
  7.2 5.3 copy-start.6
  7.2 6.0 copy-start.42
  7.2 6.6 copy-start.40
  7.2 6.6 copy-start.41
  7.2 105.7 %all-gather.9.cloned.1.call-start = ((), (), s32[]{:S(2)}) async-start(), calls=%async_computation.8 | async-start | bytes 7077888 | tf_op jit(solution)/shard_map/all_gather | solution.py:110
  9.7 153.8 %all-gather.11.cloned.1.call-start = ((), (), s32[]{:S(2)}) async-start(), calls=%async_computation.9 | async-start | bytes 2359296 | tf_op jit(solution)/shard_map/all_gather | solution.py:111
  10.5 241.7 %all-reduce.8.cloned.1.call-start = ((), (), s32[]{:S(2)}) async-start(), calls=%async_computation.10 | async-start | bytes 8388608 | tf_op jit(solution)/shard_map/psum | solution.py:26
  12.5 107.0 %copy-start.38 = (f32[512]{0:T(512)}, f32[512]{0:T(512)S(1)}, u32[]{:S(2)}) copy-start(f32[512]{0:T(512)S(1)} %broadcast_multiply_fusion.3) | copy-start | bytes 6148
  13.8 105.7 %copy-start.43 = (f32[512]{0:T(512)}, f32[512]{0:T(512)S(1)}, u32[]{:S(2)}) copy-start(f32[512]{0:T(512)S(1)} %fusion.58) | copy-start | bytes 6148
  13.8 105.7 %copy-start.36 = (f32[1,2048]{1,0:T(1,128)}, f32[1,2048]{1,0:T(1,128)S(1)}, u32[]{:S(2)}) copy-start(f32[1,2048]{1,0:T(1,128)S(1)} %get-tuple-element.171) | copy-start | bytes 24580
  13.9 105.6 %copy-start.48 = (f32[1,2048]{1,0:T(1,128)}, f32[1,2048]{1,0:T(1,128)S(1)}, u32[]{:S(2)}) copy-start(f32[1,2048]{1,0:T(1,128)S(1)} %get-tuple-element.175) | copy-start | bytes 24580
  124.3 39.2 %copy-start.32 = (bf16[4,128,512]{2,1,0:T(8,128)(2,1)}, bf16[4,128,512]{2,1,0:T(8,128)(2,1)S(1)}, u32[]{:S(2)}) copy-start(bf16[4,128,512]{2,1,0:T(8,128)(2,1)S(1)} %fusion.45) | copy-start | bytes 1572868
  168.4 3.9 copy-start.45
  168.4 4.0 copy-start.50
  168.4 135.1 %all-gather.17.cloned.1.call-start = ((), (), s32[]{:S(2)}) async-start(), calls=%async_computation.13 | async-start | bytes 2359296 | tf_op jit(solution)/shard_map/all_gather | solution.py:112
  169.0 157.0 %all-gather.15.cloned.1.call-start = ((), (), s32[]{:S(2)}) async-start(), calls=%async_computation.12 | async-start | bytes 2621440 | tf_op jit(solution)/shard_map/all_gather | solution.py:119
  169.6 283.9 %all-gather.13.cloned.1.call-start = ((), (), s32[]{:S(2)}) async-start(), calls=%async_computation.11 | async-start | bytes 9437184 | tf_op jit(solution)/shard_map/all_gather | solution.py:113
  171.0 333.1 %all-gather.19.cloned.1.call-start = ((), (), s32[]{:S(2)}) async-start(), calls=%async_computation.14 | async-start | bytes 2359296 | tf_op jit(solution)/shard_map/all_gather | solution.py:114
  171.7 421.0 %all-reduce.10.cloned.1.call-start = ((), (), s32[]{:S(2)}) async-start(), calls=%async_computation.15 | async-start | bytes 8388608 | tf_op jit(solution)/shard_map/psum | solution.py:26
  257.8 48.5 %copy-start.28 = (bf16[512,2048]{1,0:T(8,128)(2,1)}, bf16[512,2048]{1,0:T(8,128)(2,1)S(1)}, u32[]{:S(2)}) copy-start(bf16[512,2048]{1,0:T(8,128)(2,1)S(1)} %add_convert_fusion.2) | copy-start | bytes 6291460
  306.4 153.5 %copy-start.26 = (bf16[512,512]{0,1:T(8,128)(2,1)}, bf16[512,512]{0,1:T(8,128)(2,1)S(1)}, u32[]{:S(2)}) copy-start(bf16[512,512]{0,1:T(8,128)(2,1)S(1)} %convolution_convert_fusion.9) | copy-start | bytes 1572868
  461.3 47.6 %copy-start.34 = (bf16[4,128,512]{2,1,0:T(8,128)(2,1)}, bf16[4,128,512]{2,1,0:T(8,128)(2,1)S(1)}, u32[]{:S(2)}) copy-start(bf16[4,128,512]{2,1,0:T(8,128)(2,1)S(1)} %convolution_convert_fusion.8) | copy-start | bytes 1572868
  508.9 210.6 %all-gather.21.cloned.1.call-start = ((), (), s32[]{:S(2)}) async-start(), calls=%async_computation.16 | async-start | bytes 9437184 | tf_op jit(solution)/shard_map/all_gather | solution.py:115
  509.7 334.9 %all-gather.23.cloned.1.call-start = ((), (), s32[]{:S(2)}) async-start(), calls=%async_computation.17 | async-start | bytes 9437184 | tf_op jit(solution)/shard_map/all_gather | solution.py:116
  510.2 429.7 %all-reduce.12.cloned.1.call-start = ((), (), s32[]{:S(2)}) async-start(), calls=%async_computation.18 | async-start | bytes 8388608 | tf_op jit(solution)/shard_map/psum | solution.py:26
  719.5 125.0 %copy-start.51 = (f32[2048]{0:T(1024)S(1)}, f32[2048]{0:T(1024)}, u32[]{:S(2)}) copy-start(f32[2048]{0:T(1024)} %param.30) | copy-start | bytes 24580
  856.1 199.1 %all-reduce.14.cloned.1.call-start = ((), (), s32[]{:S(2)}) async-start(), calls=%async_computation.19 | async-start | bytes 8388608 | tf_op jit(solution)/shard_map/psum | solution.py:30
  947.0 16.3 slice-start
  949.9 12.0 copy-start.10
  949.9 13.3 slice-start.1
  969.4 188.3 %all-reduce.16.cloned.1.call-start = ((), (), s32[]{:S(2)}) async-start(), calls=%async_computation.20 | async-start | bytes 8388608 | tf_op jit(solution)/shard_map/psum | solution.py:30
  1055.2 4.8 copy-start.5
  1055.2 5.9 copy-start.15
  1071.9 205.7 %all-reduce.18.cloned.1.call-start = ((), (), s32[]{:S(2)}) async-start(), calls=%async_computation.21 | async-start | bytes 8388608 | tf_op jit(solution)/shard_map/psum | solution.py:30
  1157.7 4.7 copy-start.1
  1157.7 5.9 copy-start.14
  1166.4 3.9 copy-start.3
  1191.8 158.3 %reduce-scatter.15.cloned.1.call-start = ((), (), s32[]{:S(2)}) async-start(), calls=%async_computation.25 | async-start | bytes 2359296 | tf_op jit(solution)/shard_map/reduce_scatter | solution.py:261
  1196.2 187.2 %reduce-scatter.9.cloned.1.call-start = ((), (), s32[]{:S(2)}) async-start(), calls=%async_computation.22 | async-start | bytes 2621440 | tf_op jit(solution)/shard_map/reduce_scatter | solution.py:207
  1201.5 7.3 copy-start.35
  1208.7 5.0 copy-start.33
  1208.7 247.0 %reduce-scatter.19.cloned.1.call-start = ((), (), s32[]{:S(2)}) async-start(), calls=%async_computation.27 | async-start | bytes 2359296 | tf_op jit(solution)/shard_map/reduce_scatter | solution.py:267
  1213.7 313.9 %reduce-scatter.13.cloned.1.call-start = ((), (), s32[]{:S(2)}) async-start(), calls=%async_computation.24 | async-start | bytes 2359296 | tf_op jit(solution)/shard_map/reduce_scatter | solution.py:258
  1218.6 459.5 %reduce-scatter.23.cloned.1.call-start = ((), (), s32[]{:S(2)}) async-start(), calls=%async_computation.29 | async-start | bytes 9437184 | tf_op jit(solution)/shard_map/reduce_scatter | solution.py:273
  1231.1 597.1 %reduce-scatter.21.cloned.1.call-start = ((), (), s32[]{:S(2)}) async-start(), calls=%async_computation.28 | async-start | bytes 9437184 | tf_op jit(solution)/shard_map/reduce_scatter | solution.py:270
  1242.2 707.2 %reduce-scatter.11.cloned.1.call-start = ((), (), s32[]{:S(2)}) async-start(), calls=%async_computation.23 | async-start | bytes 7077888 | tf_op jit(solution)/shard_map/reduce_scatter | solution.py:255
  1251.2 849.0 %reduce-scatter.17.cloned.1.call-start = ((), (), s32[]{:S(2)}) async-start(), calls=%async_computation.26 | async-start | bytes 9437184 | tf_op jit(solution)/shard_map/reduce_scatter | solution.py:264
  1258.5 22.4 %copy-start.47 = (f32[512]{0:T(512)S(1)}, f32[512]{0:T(512)}, u32[]{:S(2)}) copy-start(f32[512]{0:T(512)} %copy-done.46) | copy-start | bytes 6148
  (31 other events, 58.3 us)
Sparse Core Ops, SparseCore 0:
  10.6 102.1 all-gather.8
  114.9 48.5 all-gather.10
  168.5 83.6 all-reduce.7
  254.2 49.2 all-gather.16
  304.9 21.0 all-gather.14
  328.5 124.9 all-gather.12
  455.5 48.5 all-gather.18
  509.0 83.6 all-reduce.9
  594.9 124.6 all-gather.20
  721.4 123.1 all-gather.22
  856.2 83.6 all-reduce.11
  969.5 85.6 all-reduce.13
  1072.1 85.6 all-reduce.15
  1191.9 85.6 all-reduce.17
  1281.5 68.5 reduce-scatter.14
  1353.1 30.2 reduce-scatter.8
  1386.8 68.8 reduce-scatter.18
  1459.7 67.8 reduce-scatter.12
  1531.2 146.8 reduce-scatter.22
  1681.6 146.5 reduce-scatter.20
  1831.8 117.5 reduce-scatter.10
  1953.0 147.0 reduce-scatter.16
where the time goes:
time: 2120 us; the launch traced here: 2110 us
  waiting for transfers between devices  1800 us (85%)
  matrix products  151 us (7%)
  other arithmetic  65.1 us (3%)
  blocking collectives  38.6 us (2%)
  local copies, waits for them, and re-layouts  36.8 us (2%)
    psum x3, waiting for transfers between devices, heads_sum(): return lax.psum(partial_value, 'mp')  246 us
    psum x3, waiting for transfers between devices, input_sum(): return lax.psum(partial_value, 'mp')  188 us
    reduce_scatter x1, waiting for transfers between devices, on_device(): lax.psum_scatter(grad_down.astype(jnp.bfloat16), 'dp', scatter_dimension=...  149 us
    reduce_scatter x1, waiting for transfers between devices, on_device(): lax.psum_scatter(grad_ckv.astype(jnp.bfloat16), 'dp', scatter_dimension=1...  148 us
    reduce_scatter x1, waiting for transfers between devices, on_device(): lax.psum_scatter(grad_up.astype(jnp.bfloat16), 'dp', scatter_dimension=0,...  147 us
    all_gather x1, waiting for transfers between devices, on_device(): lax.all_gather(c_kv, 'dp', axis=1, tiled=True)  127 us
    all_gather x1, waiting for transfers between devices, on_device(): lax.all_gather(w_up, 'dp', axis=0, tiled=True)  120 us
    reduce_scatter x1, waiting for transfers between devices, on_device(): lax.psum_scatter(grad_qkv.astype(jnp.bfloat16), 'dp', scatter_dimension=1...  118 us
  transfers between devices with their start and end apart: 22, of which 22 were waited for; matrix products, arithmetic and copies ran while one was open for 7% of the time, Pallas kernels for 0%

commit v1 on v0

--- a/solution.py
+++ b/solution.py
@@ -6,6 +6,36 @@
 HD = 128
 eps = 1e-05
 masked = -1e30
+
+
+def refer_the_slots(inner_x, dim_i):
+    inner_x = jnp.moveaxis(inner_x, 0, dim_i)
+    seen_now = inner_x.shape
+    w1 = inner_x.reshape(
+        *seen_now[:dim_i], seen_now[dim_i] * seen_now[dim_i + 1], *seen_now[dim_i + 2 :]
+    )
+    return w1
+
+
+def bind_the_teams(my_data, net_axis, ndim_at):
+    parts_n = lax.axis_size(net_axis)
+    heap = []
+    for c in tuple(range(parts_n)):
+        heap.append((c, (c + 1) % parts_n))
+    log = []
+    for kk, u in heap:
+        log.append((u, kk))
+    now, y_new = ([], [])
+    for b in [*range(parts_n - 1)]:
+        if b % 2 == 0:
+            now.append(lax.ppermute(now[-1] if now else my_data, net_axis, heap))
+        else:
+            y_new.append(lax.ppermute(y_new[-1] if y_new else my_data, net_axis, log))
+    wide_out = jnp.stack([*now[::-1], my_data, *y_new], axis=0)
+    current_value = lax.axis_index(net_axis) - len(now)
+    wide_out = wide_out[(jnp.arange(parts_n) - current_value) % parts_n]
+    val = refer_the_slots(wide_out, ndim_at)
+    return val
 
 
 def normalize(values, gain, shift):
@@ -113,7 +143,7 @@
         lax.all_gather(c_kv, "dp", axis=1, tiled=True),
         lax.all_gather(c_out, "dp", axis=1, tiled=True),
         lax.all_gather(w_up, "dp", axis=0, tiled=True),
-        lax.all_gather(w_down, "dp", axis=1, tiled=True),
+        bind_the_teams(w_down, "dp", 1),
     )
     full_qkv, full_out, full_cq, full_ckv, full_cout, full_up, full_down = gathered
     words = lax.all_gather(text, "mp", axis=1, tiled=True)

time: 2120 us -> 2040 us (0.962)
  waiting for transfers between devices: 1800 us -> 1650 us
  starting transfers between devices: 2.9 us -> 49.7 us
  local copies, waits for them, and re-layouts: 36.8 us -> 68.3 us
    ppermute x0 -> x7, waiting for transfers between devices: none -> 131 us  [the longest x4 119 us: bind_the_teams(): now.append(lax.ppermute(now[-1] if now else my_data, net_axis, heap))]
    all_gather x1 -> x0, waiting for transfers between devices: 114 us -> none  [on_device(): lax.all_gather(w_down, 'dp', axis=1, tiled=True)]
    all_gather x1, waiting for transfers between devices: 120 us -> 32.1 us  [on_device(): lax.all_gather(w_up, 'dp', axis=0, tiled=True)]
    psum x3, waiting for transfers between devices: 246 us -> 164 us  [heads_sum(): return lax.psum(partial_value, 'mp')]
    ppermute x0 -> x7, starting transfers between devices: none -> 47.1 us  [the longest x3 40.5 us: bind_the_teams(): y_new.append(lax.ppermute(y_new[-1] if y_new else my_data, net_axis, log))]
    reduce_scatter x1, waiting for transfers between devices: 20.3 us -> 52.6 us  [on_device(): lax.psum_scatter(grad_cq.astype(jnp.bfloat16), 'dp', scatter_dimension=0,...]
    reduce_scatter x1, waiting for transfers between devices: 31.5 us -> 0.01 us  [on_device(): lax.psum_scatter(text_term.astype(jnp.bfloat16), 'mp', scatter_dimension=...]
  transfers between devices with their start and end apart: 22 -> 28, of which waited for: 22 -> 24; matrix products, arithmetic and copies ran while one was open for 7% -> 8% of each run, Pallas kernels for 0% -> 0%
where the time goes in v1:
time: 2040 us
  waiting for transfers between devices  1650 us (81%)
  matrix products  149 us (7%)
  local copies, waits for them, and re-layouts  68.3 us (3%)
  other arithmetic  64.9 us (3%)
  starting transfers between devices  49.7 us (2%)
  blocking collectives  37.6 us (2%)
    psum x3, waiting for transfers between devices, input_sum(): return lax.psum(partial_value, 'mp')  190 us
    psum x3, waiting for transfers between devices, heads_sum(): return lax.psum(partial_value, 'mp')  164 us
    reduce_scatter x1, waiting for transfers between devices, on_device(): lax.psum_scatter(grad_ckv.astype(jnp.bfloat16), 'dp', scatter_dimension=1...  148 us
    reduce_scatter x1, waiting for transfers between devices, on_device(): lax.psum_scatter(grad_up.astype(jnp.bfloat16), 'dp', scatter_dimension=0,...  148 us
    reduce_scatter x1, waiting for transfers between devices, on_device(): lax.psum_scatter(grad_down.astype(jnp.bfloat16), 'dp', scatter_dimension=...  148 us
    all_gather x1, waiting for transfers between devices, on_device(): lax.all_gather(c_kv, 'dp', axis=1, tiled=True)  127 us
    ppermute x4, waiting for transfers between devices, bind_the_teams(): now.append(lax.ppermute(now[-1] if now else my_data, net_axis, heap))  119 us
    reduce_scatter x1, waiting for transfers between devices, on_device(): lax.psum_scatter(grad_qkv.astype(jnp.bfloat16), 'dp', scatter_dimension=1...  119 us
  transfers between devices with their start and end apart: 28, of which 24 were waited for; matrix products, arithmetic and copies ran while one was open for 8% of the time, Pallas kernels for 0%

profile of v1, /device:TPU:0, one launch (start us, length us, event | category | flops | bytes accessed | tf_op | source)
XLA Modules:
  0.0 2035.1 jit_solution(12705034824884164918)
XLA Ops:
  13.9 99.0 %all-gather.8.cloned.1.call-done = bf16[3,2048,512]{1,2,0:T(8,128)(2,1)} async-done(((bf16[3,256,512]{1,2,0:T(8,128)(2,1)}), bf16[3,2048,512]{1,2,0:T(8,128)(2,1)}) %all-gather.8.cloned.1.call-update) | async-done | bytes 6291472 | tf_op jit(solution)/shard_map/all_gather | solution.py:140
  112.9 6.6 fusion.35
  124.3 39.1 %all-gather.10.cloned.1.call-done = bf16[512,2048]{1,0:T(8,128)(2,1)} async-done(((bf16[512,256]{1,0:T(8,128)(2,1)}), bf16[512,2048]{1,0:T(8,128)(2,1)}) %all-gather.10.cloned.1.call-update) | async-done | bytes 2097168 | tf_op jit(solution)/shard_map/all_gather | solution.py:141
  163.5 4.9 fusion.90
  172.2 80.0 %all-reduce.8.cloned.1.call-done = f32[512,2048]{1,0:T(8,128)} async-done(((f32[512,2048]{1,0:T(8,128)}), f32[512,2048]{1,0:T(8,128)}) %all-reduce.8.cloned.1.call-update) | async-done | bytes 4194320 | tf_op jit(solution)/shard_map/psum | solution.py:56
  257.9 45.6 %all-gather.16.cloned.1.call-done = bf16[2048,512]{1,0:T(8,128)(2,1)} async-done(((bf16[256,512]{1,0:T(8,128)(2,1)}), bf16[2048,512]{1,0:T(8,128)(2,1)}) %all-gather.16.cloned.1.call-update) | async-done | bytes 2097168 | tf_op jit(solution)/shard_map/all_gather | solution.py:142
  306.4 19.6 all-gather.14.cloned.1.call-done
  326.0 127.4 %all-gather.12.cloned.1.call-done = bf16[2,4096,512]{1,2,0:T(8,128)(2,1)} async-done(((bf16[2,512,512]{1,2,0:T(8,128)(2,1)}), bf16[2,4096,512]{1,2,0:T(8,128)(2,1)}) %all-gather.12.cloned.1.call-update) | async-done | bytes 8388624 | tf_op jit(solution)/shard_map/all_gather | solution.py:143
  453.4 6.3 fusion.46
  461.3 42.7 %all-gather.18.cloned.1.call-done = bf16[512,2048]{1,0:T(8,128)(2,1)} async-done(((bf16[512,256]{1,0:T(8,128)(2,1)}), bf16[512,2048]{1,0:T(8,128)(2,1)}) %all-gather.18.cloned.1.call-update) | async-done | bytes 2097168 | tf_op jit(solution)/shard_map/all_gather | solution.py:144
  504.0 4.8 fusion.91
  511.5 25.3 %collective-permute-done = bf16[2048,256]{1,0:T(8,128)(2,1)S(1)} collective-permute-done((bf16[2048,256]{1,0:T(8,128)(2,1)S(1)}, bf16[2048,256]{1,0:T(8,128)(2,1)S(1)}, u32[]{:S(2)}, u32[]{:S(2)}) %collective-permute-start) | collective-permute-done | bytes 1048608 | tf_op jit(solution)/shard_map/ppermute | solution.py:31
  536.8 4.7 collective-permute-start.4
  541.5 39.2 %collective-permute-done.1 = bf16[2048,256]{1,0:T(8,128)(2,1)S(1)} collective-permute-done((bf16[2048,256]{1,0:T(8,128)(2,1)S(1)}, bf16[2048,256]{1,0:T(8,128)(2,1)S(1)}, u32[]{:S(2)}, u32[]{:S(2)}) %collective-permute-start.1) | collective-permute-done | bytes 1048608 | tf_op jit(solution)/shard_map/ppermute | solution.py:31
  583.2 23.0 %collective-permute-start.5 = (bf16[2048,256]{1,0:T(8,128)(2,1)}, bf16[2048,256]{1,0:T(8,128)(2,1)}, u32[]{:S(2)}, u32[]{:S(2)}) collective-permute-start(bf16[2048,256]{1,0:T(8,128)(2,1)} %collective-permute-done.4), channel_id=1, source_target_pairs={{4,0},{8,4},{12,8},{16,12},{20,16},{24,20},{28,24},{0,28},{5,1},{9... | collective-permute-start | bytes 3145736 | tf_op jit(solution)/shard_map/ppermute | solution.py:33
  606.3 31.4 %collective-permute-done.2 = bf16[2048,256]{1,0:T(8,128)(2,1)} collective-permute-done((bf16[2048,256]{1,0:T(8,128)(2,1)S(1)}, bf16[2048,256]{1,0:T(8,128)(2,1)}, u32[]{:S(2)}, u32[]{:S(2)}) %collective-permute-start.2) | collective-permute-done | bytes 1048608 | tf_op jit(solution)/shard_map/ppermute | solution.py:31
  640.3 12.1 collective-permute-done.5
  652.3 12.8 collective-permute-start.6
  665.1 23.5 %collective-permute-done.3 = bf16[2048,256]{1,0:T(8,128)(2,1)} collective-permute-done((bf16[2048,256]{1,0:T(8,128)(2,1)}, bf16[2048,256]{1,0:T(8,128)(2,1)}, u32[]{:S(2)}, u32[]{:S(2)}) %collective-permute-start.3) | collective-permute-done | bytes 1048608 | tf_op jit(solution)/shard_map/ppermute | solution.py:31
  702.1 8.2 gather_fusion
  710.2 11.5 copy.96
  728.2 32.1 %all-gather.20.cloned.1.call-done = bf16[2048,2048]{1,0:T(8,128)(2,1)} async-done(((bf16[256,2048]{1,0:T(8,128)(2,1)}), bf16[2048,2048]{1,0:T(8,128)(2,1)}) %all-gather.20.cloned.1.call-update) | async-done | bytes 8388624 | tf_op jit(solution)/shard_map/all_gather | solution.py:145
  760.3 8.3 fusion.71
  770.7 9.9 fusion.70
  780.9 84.4 %all-reduce.12.cloned.1.call-done = f32[512,2048]{1,0:T(8,128)} async-done(((f32[512,2048]{1,0:T(8,128)}), f32[512,2048]{1,0:T(8,128)}) %all-reduce.12.cloned.1.call-update) | async-done | bytes 4194320 | tf_op jit(solution)/shard_map/psum | solution.py:56
  875.4 12.4 fusion.89
  887.8 7.8 fusion.92
  895.9 85.5 %all-reduce.14.cloned.1.call-done = f32[512,2048]{1,0:T(8,128)} async-done(((f32[512,2048]{1,0:T(8,128)}), f32[512,2048]{1,0:T(8,128)}) %all-reduce.14.cloned.1.call-update) | async-done | bytes 4194320 | tf_op jit(solution)/shard_map/psum | solution.py:60
  998.5 85.5 %all-reduce.16.cloned.1.call-done = f32[512,2048]{1,0:T(8,128)} async-done(((f32[512,2048]{1,0:T(8,128)}), f32[512,2048]{1,0:T(8,128)}) %all-reduce.16.cloned.1.call-update) | async-done | bytes 4194320 | tf_op jit(solution)/shard_map/psum | solution.py:60
  1084.0 4.6 multiply_reduce_fusion.1
  1109.4 8.7 convolution_bitcast_fusion.1
  1123.7 7.4 fusion.4
  1133.9 5.0 convolution_convert_fusion.2
  1139.0 5.1 convolution_convert_fusion.4
  1144.2 7.1 convert_bitcast_fusion.1
  1151.6 11.0 convolution_convert_fusion.1
  1162.7 12.4 convolution_convert_fusion
  1175.3 7.2 convert_bitcast_fusion
  1184.7 19.2 all-reduce.18.cloned.1.call-done
  1209.4 37.6 %all-reduce = (bf16[4,2048]{1,0:T(4,128)(2,1)S(1)}, bf16[4,2048]{1,0:T(4,128)(2,1)S(1)}, bf16[3,2048]{1,0:T(4,128)(2,1)S(1)}, bf16[2048]{0:T(1024)(128)(2,1)S(1)}) all-reduce(bf16[4,2048]{1,0:T(4,128)(2,1)S(1)} %get-tuple-element.218, bf16[4,2048]{1,0:T(4,128)(2,1)S(1)} %get-tuple-element.219, ...), channel_id=1, replica_groups=mesh['dp'=8,'mp'=4] {'dp'}, use_global_device_ids=true, to_apply=%region_40.41 | all-reduce | flops 24576 | bytes 98304 | tf_op jit(solution)/shard_map/psum | solution.py:279
  1249.5 5.6 add_add_fusion.4
  1257.2 52.6 %reduce-scatter.15.cloned.1.call-done = bf16[256,512]{1,0:T(8,128)(2,1)} async-done(((bf16[2048,512]{1,0:T(8,128)(2,1)}), bf16[256,512]{1,0:T(8,128)(2,1)}) %reduce-scatter.15.cloned.1.call-update) | async-done | bytes 262160 | tf_op jit(solution)/shard_map/reduce_scatter | solution.py:291
  1311.7 69.5 %reduce-scatter.19.cloned.1.call-done = bf16[512,256]{1,0:T(8,128)(2,1)} async-done(((bf16[512,2048]{1,0:T(8,128)(2,1)}), bf16[512,256]{1,0:T(8,128)(2,1)}) %reduce-scatter.19.cloned.1.call-update) | async-done | bytes 262160 | tf_op jit(solution)/shard_map/reduce_scatter | solution.py:297
  1382.9 70.1 %reduce-scatter.13.cloned.1.call-done = bf16[512,256]{1,0:T(8,128)(2,1)} async-done(((bf16[512,2048]{1,0:T(8,128)(2,1)}), bf16[512,256]{1,0:T(8,128)(2,1)}) %reduce-scatter.13.cloned.1.call-update) | async-done | bytes 262160 | tf_op jit(solution)/shard_map/reduce_scatter | solution.py:288
  1454.8 119.2 %reduce-scatter.11.cloned.1.call-done = bf16[3,256,512]{1,2,0:T(8,128)(2,1)} async-done(((bf16[3,2048,512]{1,2,0:T(8,128)(2,1)}), bf16[3,256,512]{1,2,0:T(8,128)(2,1)}) %reduce-scatter.11.cloned.1.call-update) | async-done | bytes 786448 | tf_op jit(solution)/shard_map/reduce_scatter | solution.py:285
  1576.5 147.8 %reduce-scatter.21.cloned.1.call-done = bf16[256,2048]{1,0:T(8,128)(2,1)} async-done(((bf16[2048,2048]{1,0:T(8,128)(2,1)}), bf16[256,2048]{1,0:T(8,128)(2,1)}) %reduce-scatter.21.cloned.1.call-update) | async-done | bytes 1048592 | tf_op jit(solution)/shard_map/reduce_scatter | solution.py:300
  1727.1 147.7 %reduce-scatter.23.cloned.1.call-done = bf16[2048,256]{1,0:T(8,128)(2,1)} async-done(((bf16[2048,2048]{1,0:T(8,128)(2,1)}), bf16[2048,256]{1,0:T(8,128)(2,1)}) %reduce-scatter.23.cloned.1.call-update) | async-done | bytes 1048592 | tf_op jit(solution)/shard_map/reduce_scatter | solution.py:303
  1877.5 147.9 %reduce-scatter.17.cloned.1.call-done = bf16[2,512,512]{1,2,0:T(8,128)(2,1)} async-done(((bf16[2,4096,512]{1,2,0:T(8,128)(2,1)}), bf16[2,512,512]{1,2,0:T(8,128)(2,1)}) %reduce-scatter.17.cloned.1.call-update) | async-done | bytes 1048592 | tf_op jit(solution)/shard_map/reduce_scatter | solution.py:294
  (287 shorter events, 140.4 us)
Async XLA Ops:
  7.2 6.6 copy-start.48
  7.2 105.7 %all-gather.8.cloned.1.call-start = ((), (), s32[]{:S(2)}) async-start(), calls=%async_computation.8 | async-start | bytes 7077888 | tf_op jit(solution)/shard_map/all_gather | solution.py:140
  9.7 153.8 %all-gather.10.cloned.1.call-start = ((), (), s32[]{:S(2)}) async-start(), calls=%async_computation.9 | async-start | bytes 2359296 | tf_op jit(solution)/shard_map/all_gather | solution.py:141
  10.5 241.7 %all-reduce.8.cloned.1.call-start = ((), (), s32[]{:S(2)}) async-start(), calls=%async_computation.10 | async-start | bytes 8388608 | tf_op jit(solution)/shard_map/psum | solution.py:56
  12.5 107.0 %copy-start.45 = (f32[512]{0:T(512)}, f32[512]{0:T(512)S(1)}, u32[]{:S(2)}) copy-start(f32[512]{0:T(512)S(1)} %broadcast_multiply_fusion.3) | copy-start | bytes 6148
  13.8 105.7 %copy-start.50 = (f32[512]{0:T(512)}, f32[512]{0:T(512)S(1)}, u32[]{:S(2)}) copy-start(f32[512]{0:T(512)S(1)} %fusion.58) | copy-start | bytes 6148
  13.8 105.7 %copy-start.55 = (f32[1,2048]{1,0:T(1,128)}, f32[1,2048]{1,0:T(1,128)S(1)}, u32[]{:S(2)}) copy-start(f32[1,2048]{1,0:T(1,128)S(1)} %get-tuple-element.203) | copy-start | bytes 24580
  13.9 105.6 %copy-start.43 = (f32[1,2048]{1,0:T(1,128)}, f32[1,2048]{1,0:T(1,128)S(1)}, u32[]{:S(2)}) copy-start(f32[1,2048]{1,0:T(1,128)S(1)} %get-tuple-element.199) | copy-start | bytes 24580
  124.3 39.1 %copy-start.41 = (bf16[4,128,512]{2,1,0:T(8,128)(2,1)}, bf16[4,128,512]{2,1,0:T(8,128)(2,1)S(1)}, u32[]{:S(2)}) copy-start(bf16[4,128,512]{2,1,0:T(8,128)(2,1)S(1)} %fusion.45) | copy-start | bytes 1572868
  168.4 135.1 %all-gather.16.cloned.1.call-start = ((), (), s32[]{:S(2)}) async-start(), calls=%async_computation.13 | async-start | bytes 2359296 | tf_op jit(solution)/shard_map/all_gather | solution.py:142
  169.0 157.0 %all-gather.14.cloned.1.call-start = ((), (), s32[]{:S(2)}) async-start(), calls=%async_computation.12 | async-start | bytes 2621440 | tf_op jit(solution)/shard_map/all_gather | solution.py:149
  169.6 283.9 %all-gather.12.cloned.1.call-start = ((), (), s32[]{:S(2)}) async-start(), calls=%async_computation.11 | async-start | bytes 9437184 | tf_op jit(solution)/shard_map/all_gather | solution.py:143
  171.0 333.1 %all-gather.18.cloned.1.call-start = ((), (), s32[]{:S(2)}) async-start(), calls=%async_computation.14 | async-start | bytes 2359296 | tf_op jit(solution)/shard_map/all_gather | solution.py:144
  171.7 550.0 %all-reduce.10.cloned.1.call-start = ((), (), s32[]{:S(2)}) async-start(), calls=%async_computation.15 | async-start | bytes 8388608 | tf_op jit(solution)/shard_map/psum | solution.py:56
  257.8 48.5 %copy-start.29 = (bf16[512,2048]{1,0:T(8,128)(2,1)}, bf16[512,2048]{1,0:T(8,128)(2,1)S(1)}, u32[]{:S(2)}) copy-start(bf16[512,2048]{1,0:T(8,128)(2,1)S(1)} %add_convert_fusion.2) | copy-start | bytes 6291460
  306.3 153.5 %copy-start.27 = (bf16[512,512]{0,1:T(8,128)(2,1)}, bf16[512,512]{0,1:T(8,128)(2,1)S(1)}, u32[]{:S(2)}) copy-start(bf16[512,512]{0,1:T(8,128)(2,1)S(1)} %convolution_convert_fusion.9) | copy-start | bytes 1572868
  461.3 42.7 %copy-start.42 = (bf16[4,128,512]{2,1,0:T(8,128)(2,1)}, bf16[4,128,512]{2,1,0:T(8,128)(2,1)S(1)}, u32[]{:S(2)}) copy-start(bf16[4,128,512]{2,1,0:T(8,128)(2,1)S(1)} %convolution_convert_fusion.8) | copy-start | bytes 1572868
  508.9 251.5 %all-gather.20.cloned.1.call-start = ((), (), s32[]{:S(2)}) async-start(), calls=%async_computation.16 | async-start | bytes 9437184 | tf_op jit(solution)/shard_map/all_gather | solution.py:145
  509.6 355.7 %all-reduce.12.cloned.1.call-start = ((), (), s32[]{:S(2)}) async-start(), calls=%async_computation.17 | async-start | bytes 8388608 | tf_op jit(solution)/shard_map/psum | solution.py:56
  510.1 26.8 %collective-permute-start = (bf16[2048,256]{1,0:T(8,128)(2,1)S(1)}, bf16[2048,256]{1,0:T(8,128)(2,1)S(1)}, u32[]{:S(2)}, u32[]{:S(2)}) collective-permute-start(bf16[2048,256]{1,0:T(8,128)(2,1)S(1)} %copy-done.33), channel_id=1, source_target_pairs={{0,4},{4,8},{8,12},{12,16},{16,20},{20,24},{24,28},{28,0},{1,5},{5... | collective-permute-start | bytes 3145736 | tf_op jit(solution)/shard_map/ppermute | solution.py:31
  536.8 46.4 %copy-start.34 = (bf16[2048,256]{1,0:T(8,128)(2,1)}, bf16[2048,256]{1,0:T(8,128)(2,1)S(1)}, u32[]{:S(2)}) copy-start(bf16[2048,256]{1,0:T(8,128)(2,1)S(1)} %collective-permute-done) | copy-start | bytes 3145732
  536.8 43.9 %collective-permute-start.1 = (bf16[2048,256]{1,0:T(8,128)(2,1)S(1)}, bf16[2048,256]{1,0:T(8,128)(2,1)S(1)}, u32[]{:S(2)}, u32[]{:S(2)}) collective-permute-start(bf16[2048,256]{1,0:T(8,128)(2,1)S(1)} %collective-permute-done), channel_id=1, source_target_pairs={{0,4},{4,8},{8,12},{12,16},{16,20},{20,24},{24,28},{28,0},{1,5},{5... | collective-permute-start | bytes 3145736 | tf_op jit(solution)/shard_map/ppermute | solution.py:31
  536.8 46.4 %collective-permute-start.4 = (bf16[2048,256]{1,0:T(8,128)(2,1)S(1)}, bf16[2048,256]{1,0:T(8,128)(2,1)}, u32[]{:S(2)}, u32[]{:S(2)}) collective-permute-start(bf16[2048,256]{1,0:T(8,128)(2,1)S(1)} %copy-done.33), channel_id=1, source_target_pairs={{4,0},{8,4},{12,8},{16,12},{20,16},{24,20},{28,24},{0,28},{5,1},{9... | collective-permute-start | bytes 3145736 | tf_op jit(solution)/shard_map/ppermute | solution.py:33
  580.8 25.5 %copy-start.36 = (bf16[2048,256]{1,0:T(8,128)(2,1)}, bf16[2048,256]{1,0:T(8,128)(2,1)S(1)}, u32[]{:S(2)}) copy-start(bf16[2048,256]{1,0:T(8,128)(2,1)S(1)} %collective-permute-done.1) | copy-start | bytes 3145732
  580.8 56.9 %collective-permute-start.2 = (bf16[2048,256]{1,0:T(8,128)(2,1)S(1)}, bf16[2048,256]{1,0:T(8,128)(2,1)}, u32[]{:S(2)}, u32[]{:S(2)}) collective-permute-start(bf16[2048,256]{1,0:T(8,128)(2,1)S(1)} %collective-permute-done.1), channel_id=1, source_target_pairs={{0,4},{4,8},{8,12},{12,16},{16,20},{20,24},{24,28},{28,0},{1,5},{5... | collective-permute-start | bytes 3145736 | tf_op jit(solution)/shard_map/ppermute | solution.py:31
  583.2 69.1 %collective-permute-start.5 = (bf16[2048,256]{1,0:T(8,128)(2,1)}, bf16[2048,256]{1,0:T(8,128)(2,1)}, u32[]{:S(2)}, u32[]{:S(2)}) collective-permute-start(bf16[2048,256]{1,0:T(8,128)(2,1)} %collective-permute-done.4), channel_id=1, source_target_pairs={{4,0},{8,4},{12,8},{16,12},{20,16},{24,20},{28,24},{0,28},{5,1},{9... | collective-permute-start | bytes 3145736 | tf_op jit(solution)/shard_map/ppermute | solution.py:33
  637.7 50.9 %collective-permute-start.3 = (bf16[2048,256]{1,0:T(8,128)(2,1)}, bf16[2048,256]{1,0:T(8,128)(2,1)}, u32[]{:S(2)}, u32[]{:S(2)}) collective-permute-start(bf16[2048,256]{1,0:T(8,128)(2,1)} %collective-permute-done.2), channel_id=1, source_target_pairs={{0,4},{4,8},{8,12},{12,16},{16,20},{20,24},{24,28},{28,0},{1,5},{5... | collective-permute-start | bytes 3145736 | tf_op jit(solution)/shard_map/ppermute | solution.py:31
  640.3 52.9 %copy-start.37 = (bf16[2048,256]{1,0:T(8,128)(2,1)S(1)}, bf16[2048,256]{1,0:T(8,128)(2,1)}, u32[]{:S(2)}) copy-start(bf16[2048,256]{1,0:T(8,128)(2,1)} %copy-done.36) | copy-start | bytes 3145732
  640.3 54.0 %copy-start.35 = (bf16[2048,256]{1,0:T(8,128)(2,1)S(1)}, bf16[2048,256]{1,0:T(8,128)(2,1)}, u32[]{:S(2)}) copy-start(bf16[2048,256]{1,0:T(8,128)(2,1)} %copy-done.34) | copy-start | bytes 3145732
  652.3 48.6 %collective-permute-start.6 = (bf16[2048,256]{1,0:T(8,128)(2,1)}, bf16[2048,256]{1,0:T(8,128)(2,1)S(1)}, u32[]{:S(2)}, u32[]{:S(2)}) collective-permute-start(bf16[2048,256]{1,0:T(8,128)(2,1)} %collective-permute-done.5), channel_id=1, source_target_pairs={{4,0},{8,4},{12,8},{16,12},{20,16},{24,20},{28,24},{0,28},{5,1},{9... | collective-permute-start | bytes 3145736 | tf_op jit(solution)/shard_map/ppermute | solution.py:33
  760.3 10.4 copy-start.58
  780.7 200.7 %all-reduce.14.cloned.1.call-start = ((), (), s32[]{:S(2)}) async-start(), calls=%async_computation.18 | async-start | bytes 8388608 | tf_op jit(solution)/shard_map/psum | solution.py:60
  872.4 15.4 slice-start.2
  875.4 12.4 copy-start.10
  875.4 12.4 slice-start.3
  895.6 188.3 %all-reduce.16.cloned.1.call-start = ((), (), s32[]{:S(2)}) async-start(), calls=%async_computation.19 | async-start | bytes 8388608 | tf_op jit(solution)/shard_map/psum | solution.py:60
  998.2 205.7 %all-reduce.18.cloned.1.call-start = ((), (), s32[]{:S(2)}) async-start(), calls=%async_computation.20 | async-start | bytes 8388608 | tf_op jit(solution)/shard_map/psum | solution.py:60
  1118.1 137.0 %reduce-scatter.9.cloned.1.call-start = ((), (), s32[]{:S(2)}) async-start(), calls=%async_computation.21 | async-start | bytes 2621440 | tf_op jit(solution)/shard_map/reduce_scatter | solution.py:237
  1123.7 7.5 copy-start.22
  1123.7 7.5 copy-start.30
  1131.1 178.8 %reduce-scatter.15.cloned.1.call-start = ((), (), s32[]{:S(2)}) async-start(), calls=%async_computation.24 | async-start | bytes 2359296 | tf_op jit(solution)/shard_map/reduce_scatter | solution.py:291
  1133.9 247.3 %reduce-scatter.19.cloned.1.call-start = ((), (), s32[]{:S(2)}) async-start(), calls=%async_computation.26 | async-start | bytes 2359296 | tf_op jit(solution)/shard_map/reduce_scatter | solution.py:297
  1139.0 314.0 %reduce-scatter.13.cloned.1.call-start = ((), (), s32[]{:S(2)}) async-start(), calls=%async_computation.23 | async-start | bytes 2359296 | tf_op jit(solution)/shard_map/reduce_scatter | solution.py:288
  1144.1 429.8 %reduce-scatter.11.cloned.1.call-start = ((), (), s32[]{:S(2)}) async-start(), calls=%async_computation.22 | async-start | bytes 7077888 | tf_op jit(solution)/shard_map/reduce_scatter | solution.py:285
  1151.4 572.9 %reduce-scatter.21.cloned.1.call-start = ((), (), s32[]{:S(2)}) async-start(), calls=%async_computation.27 | async-start | bytes 9437184 | tf_op jit(solution)/shard_map/reduce_scatter | solution.py:300
  1162.6 712.2 %reduce-scatter.23.cloned.1.call-start = ((), (), s32[]{:S(2)}) async-start(), calls=%async_computation.28 | async-start | bytes 9437184 | tf_op jit(solution)/shard_map/reduce_scatter | solution.py:303
  1175.0 850.4 %reduce-scatter.17.cloned.1.call-start = ((), (), s32[]{:S(2)}) async-start(), calls=%async_computation.25 | async-start | bytes 9437184 | tf_op jit(solution)/shard_map/reduce_scatter | solution.py:294
  1182.5 24.6 %copy-start.54 = (f32[512]{0:T(512)S(1)}, f32[512]{0:T(512)}, u32[]{:S(2)}) copy-start(f32[512]{0:T(512)} %copy-done.53) | copy-start | bytes 6148
  (44 other events, 137.2 us)
Sparse Core Ops, SparseCore 0:
  10.6 102.1 all-gather.7
  114.9 48.5 all-gather.9
  168.5 83.6 all-reduce.7
  254.2 49.2 all-gather.15
  304.9 21.0 all-gather.13
  328.5 124.9 all-gather.11
  455.5 48.5 all-gather.17
  509.0 83.6 all-reduce.9
  594.8 165.4 all-gather.19
  780.8 84.4 all-reduce.11
  895.7 85.6 all-reduce.13
  998.3 85.6 all-reduce.15
  1118.2 85.6 all-reduce.17
  1206.9 31.2 reduce-scatter.8
  1241.6 68.2 reduce-scatter.14
  1313.3 67.8 reduce-scatter.18
  1385.1 67.8 reduce-scatter.12
  1456.5 117.4 reduce-scatter.10
  1577.6 146.7 reduce-scatter.20
  1727.8 146.9 reduce-scatter.22
  1878.4 146.9 reduce-scatter.16
